TPU v7x, 32 devices: a whole 2x2x4 slice. The times are simulated.
32 devices in a mesh: seq: 16 (over z, y, core), head: 2 (over x).
Axes of the slice: x: 2, y: 2, z: 4, core: 2. Of those that a mesh axis runs over, the one named last changes fastest.
Arguments:
- tokens: bfloat16 [512, 2048], P('seq', 'head'), may hold values from -6 to 6
- ln1_gain: float32 [2048], replicated, may hold values from 0.1 to 1.9
- ln1_shift: float32 [2048], replicated, may hold values from -1.75 to 1.75
- ln2_gain: float32 [2048], replicated, may hold values from 0.1 to 1.9
- ln2_shift: float32 [2048], replicated, may hold values from -1.75 to 1.75
- w_qkv: bfloat16 [2048, 3, 2048], P(None, None, 'head'), may hold values from -0.125 to 0.125
- b_qkv: float32 [3, 2048], P(None, 'head'), may hold values from -3 to 3
- w_dense: bfloat16 [2048, 2048], P('head'), may hold values from -0.125 to 0.125
- b_dense: float32 [2048], P('head'), may hold values from -1.75 to 1.75
- w_up: bfloat16 [2048, 4096], P(None, 'head'), may hold values from -0.125 to 0.125
- b_up: float32 [4096], P('head'), may hold values from -3 to 3
- w_down: bfloat16 [4096, 2048], P('head'), may hold values from -0.09375 to 0.09375
- b_down: float32 [2048], P('head'), may hold values from -1.75 to 1.75
- keys_short: bfloat16 [512, 64, 2048], P('seq', None, 'head'), may hold values from -210 to 210
- values_short: bfloat16 [512, 64, 2048], P('seq', None, 'head'), may hold values from -16 to 16
- keys_long: bfloat16 [32768, 2048], P('seq', 'head'), may hold values from -210 to 210
- values_long: bfloat16 [32768, 2048], P('seq', 'head'), may hold values from -16 to 16
- lengths: int32 [512], replicated, may hold values from 16 to 8192, as said below
- slot_request: int32 [512], replicated, may hold values from 0 to 511, as said below
- piece_map: int32 [16], replicated, may hold values from 0 to 15, each once
Outputs:
- layer_out: bfloat16 [512, 2048], P('seq', 'head')
Inputs may be any that keep to these rules, and one draw needn't show every extreme that they name: `lengths`: requests 0 to 3 hold more than 4096 positions, one of them exactly 8192; every other request holds 16 to 64 positions, one of them exactly 64. `slot_request`: A permutation of the requests; slot s lies on index s // 32 of seq. The requests 32 h to 32 h + 31 are served in 8 groups of exactly 4 on as many different indices of seq. Rows 2048 b to 2048 b + 2047 of keys_long and values_long hold positions (piece_map[b] % 4) * 2048 onwards of the cache of request piece_map[b] // 4.
All inputs are finite; a program needn't handle non-finite values.
Results may differ from a plain program's by a relative error of at most 0.0095.
Values may be sent and summed in bfloat16 or wider, within the bound.
A program may use at most 192 MiB of HBM per device.

v0:
```python
import jax
import jax.numpy as jnp
from jax import lax
from jax.sharding import PartitionSpec as P

HD = 256
ROT = 64
LONGS = 4
epsilon = 1e-05
very_low = -1e30


def merged(array, axis, combine):
    everything = jax.tree.map(lambda part: lax.all_gather(part, axis), array)
    first = jax.tree.map(lambda part: part[0], everything)

    def hop(k, so_far):
        return combine(so_far, jax.tree.map(lambda part: part[k], everything))

    return lax.fori_loop(1, lax.axis_size(axis), hop, first)


def layer_norm(values, gain, shift):
    center = jnp.mean(values, axis=-1, keepdims=True)
    offset = values - center
    spread = jnp.mean(offset * offset, axis=-1, keepdims=True)
    return offset * lax.rsqrt(spread + epsilon) * gain + shift


def rotary(values, position):
    half_rot = ROT // 2
    frequency = jnp.power(10000.0, -2.0 * jnp.arange(half_rot, dtype=jnp.float32) / ROT)
    angles = position.astype(jnp.float32)[:, None] * frequency[None, :]
    cosine = jnp.cos(angles)[:, None, :]
    sine_of = jnp.sin(angles)[:, None, :]
    leading = values[..., :half_rot]
    trailing = values[..., half_rot:ROT]
    return jnp.concatenate(
        [
            leading * cosine - trailing * sine_of,
            trailing * cosine + leading * sine_of,
            values[..., ROT:],
        ],
        axis=-1,
    )


def attend(queries, key_rows, value_rows, usable):
    scores = jnp.einsum(
        "rhc,rthc->rht", queries, key_rows, preferred_element_type=jnp.float32
    ) * HD ** (-0.5)
    masked = jnp.where(usable[:, None, :], scores, very_low)
    summit = jnp.max(masked, axis=-1)
    weights = jnp.where(usable[:, None, :], jnp.exp(masked - summit[..., None]), 0.0)
    amount = jnp.sum(weights, axis=-1)
    mixed = jnp.einsum(
        "rht,rthc->rhc",
        weights.astype(jnp.bfloat16),
        value_rows,
        preferred_element_type=jnp.float32,
    )
    return (summit, amount, mixed)


def combine_partials(first_part, second_part):
    top_first, total_first, out_first = first_part
    top_second, total_second, out_second = second_part
    summit = jnp.maximum(top_first, top_second)
    scale_first = jnp.exp(top_first - summit)
    scale_second = jnp.exp(top_second - summit)
    total_both = total_first * scale_first + total_second * scale_second
    out_both = out_first * scale_first[..., None] + out_second * scale_second[..., None]
    return (summit, total_both, out_both)


def local(
    tokens,
    ln1_gain,
    ln1_shift,
    ln2_gain,
    ln2_shift,
    w_qkv,
    b_qkv,
    w_dense,
    b_dense,
    w_up,
    b_up,
    w_down,
    b_down,
    keys_short,
    values_short,
    keys_long,
    values_long,
    lengths,
    slot_request,
    piece_map,
):
    slot_rows, part_width = tokens.shape
    seq_count = lax.axis_size("seq")
    seq_place = lax.axis_index("seq")
    request_count = slot_request.shape[0]
    heads_here = part_width // HD
    my_requests = lax.dynamic_slice_in_dim(slot_request, seq_place * slot_rows, slot_rows)
    shard_rows = lax.all_gather(tokens, "seq", axis=0, tiled=True)
    row_ids = jnp.arange(shard_rows.shape[0], dtype=jnp.int32)
    selector = (my_requests[:, None] == row_ids[None, :]).astype(jnp.bfloat16)
    own_cols = jnp.dot(selector, shard_rows, preferred_element_type=jnp.float32).astype(
        jnp.bfloat16
    )
    full_rows = lax.all_gather(own_cols, "head", axis=1, tiled=True)
    resident = full_rows.astype(jnp.float32)
    normed_attn = layer_norm(resident, ln1_gain, ln1_shift).astype(jnp.bfloat16)
    normed_mlp = layer_norm(resident, ln2_gain, ln2_shift).astype(jnp.bfloat16)
    projected = jnp.dot(
        normed_attn,
        w_qkv.reshape(w_qkv.shape[0], 3 * part_width),
        preferred_element_type=jnp.float32,
    )
    projected = projected.reshape(slot_rows, 3, part_width) + b_qkv[None]
    request_ids = jnp.arange(request_count, dtype=jnp.int32)
    my_lengths = jnp.sum(
        jnp.where(my_requests[:, None] == request_ids[None, :], lengths[None, :], 0), axis=1
    )
    queries = rotary(projected[:, 0].reshape(slot_rows, heads_here, HD), my_lengths).astype(
        jnp.bfloat16
    )
    new_keys = rotary(projected[:, 1].reshape(slot_rows, heads_here, HD), my_lengths).astype(
        jnp.bfloat16
    )
    new_values = projected[:, 2].reshape(slot_rows, heads_here, HD).astype(jnp.bfloat16)
    long_hits = my_requests[:, None] == jnp.arange(LONGS, dtype=jnp.int32)[None, :]
    long_part = jnp.sum(
        jnp.where(long_hits[:, :, None, None], queries.astype(jnp.float32)[:, None], 0.0), axis=0
    )
    long_queries = lax.psum(long_part, "seq")
    short_max = keys_short.shape[1]
    short_usable = (jnp.arange(short_max, dtype=jnp.int32)[None, :] < my_lengths[:, None]) & (
        my_lengths <= short_max
    )[:, None]
    short_keys = keys_short.reshape(slot_rows, short_max, heads_here, HD)
    short_vals = values_short.reshape(slot_rows, short_max, heads_here, HD)
    short_top, short_total, short_out = attend(queries, short_keys, short_vals, short_usable)
    own_score = jnp.sum(
        queries.astype(jnp.float32) * new_keys.astype(jnp.float32), axis=-1
    ) * HD ** (-0.5)
    piece_count = seq_count // LONGS
    my_piece = lax.dynamic_slice_in_dim(piece_map, seq_place, 1)[0]
    long_owner = my_piece // piece_count
    piece_index = my_piece % piece_count
    long_pick = jnp.arange(LONGS, dtype=jnp.int32) == long_owner
    piece_query = jnp.sum(jnp.where(long_pick[:, None, None], long_queries, 0.0), axis=0).astype(
        jnp.bfloat16
    )
    long_length = jnp.sum(jnp.where(long_pick, lengths[:LONGS], 0))
    piece_len = keys_long.shape[0]
    positions = piece_index * piece_len + jnp.arange(piece_len, dtype=jnp.int32)
    piece_usable = (positions < long_length)[None, :]
    piece_keys = keys_long.reshape(1, piece_len, heads_here, HD)
    piece_vals = values_long.reshape(1, piece_len, heads_here, HD)
    piece_top, piece_total, piece_out = attend(
        piece_query[None], piece_keys, piece_vals, piece_usable
    )
    spread_top = jnp.where(long_pick[:, None], piece_top, very_low)
    spread_total = jnp.where(long_pick[:, None], piece_total, 0.0)
    spread_out = jnp.where(long_pick[:, None, None], piece_out, 0.0)
    long_top, long_total, long_out = merged(
        (spread_top, spread_total, spread_out), "seq", combine_partials
    )
    has_long = jnp.any(long_hits, axis=1)
    mine_top = jnp.where(
        has_long[:, None],
        jnp.sum(jnp.where(long_hits[:, :, None], long_top[None], 0.0), axis=1),
        very_low,
    )
    mine_total = jnp.sum(jnp.where(long_hits[:, :, None], long_total[None], 0.0), axis=1)
    mine_out = jnp.sum(jnp.where(long_hits[:, :, None, None], long_out[None], 0.0), axis=1)
    summit = jnp.maximum(jnp.maximum(short_top, own_score), mine_top)
    short_scale = jnp.exp(short_top - summit)
    own_scale = jnp.exp(own_score - summit)
    long_scale = jnp.exp(mine_top - summit)
    denominator = short_total * short_scale + own_scale + mine_total * long_scale
    numerator = (
        short_out * short_scale[..., None]
        + new_values.astype(jnp.float32) * own_scale[..., None]
        + mine_out * long_scale[..., None]
    )
    attended = (
        (numerator / denominator[..., None]).reshape(slot_rows, part_width).astype(jnp.bfloat16)
    )
    hidden_units = jax.nn.gelu(
        jnp.dot(normed_mlp, w_up, preferred_element_type=jnp.float32) + b_up, approximate=False
    ).astype(jnp.bfloat16)
    partial_sum = jnp.dot(attended, w_dense, preferred_element_type=jnp.float32) + jnp.dot(
        hidden_units, w_down, preferred_element_type=jnp.float32
    )
    head_total = lax.psum_scatter(
        partial_sum.astype(jnp.bfloat16), "head", scatter_dimension=1, tiled=True
    ).astype(jnp.float32)
    finished = (own_cols.astype(jnp.float32) + head_total + b_dense + b_down).astype(jnp.bfloat16)
    home_ids = seq_place * slot_rows + jnp.arange(slot_rows, dtype=jnp.int32)
    selector = (slot_request[None, :] == home_ids[:, None]).astype(jnp.bfloat16)
    return jnp.dot(
        selector,
        lax.all_gather(finished, "seq", axis=0, tiled=True),
        preferred_element_type=jnp.float32,
    ).astype(jnp.bfloat16)


def solution(mesh):
    in_specs = (
        P("seq", "head"),
        P(),
        P(),
        P(),
        P(),
        P(None, None, "head"),
        P(None, "head"),
        P("head", None),
        P("head"),
        P(None, "head"),
        P("head"),
        P("head", None),
        P("head"),
        P("seq", None, "head"),
        P("seq", None, "head"),
        P("seq", "head"),
        P("seq", "head"),
        P(),
        P(),
        P(),
    )
    out_specs = P("seq", "head")
    return jax.shard_map(local, mesh=mesh, in_specs=in_specs, out_specs=out_specs, check_vma=False)
```

profile of v0, /device:TPU:0, one launch (start us, length us, event | category | flops | bytes accessed | tf_op | source)
XLA Modules:
  0.0 262.1 jit_solution(12537288334544157710)
XLA Ops:
  6.5 0.7 all-gather.3.cloned.1.call-update
  7.3 1.2 dynamic_slice.37
  11.2 17.0 %copy.30 = bf16[2048,3,1024]{0,2,1:T(8,128)(2,1)} copy(bf16[2048,3,1024]{2,0,1:T(8,128)(2,1)} %param.27) | data formatting | bytes 25165824 | tf_op args[5]
  28.2 0.1 dynamic_slice.36
  28.2 0.2 select_reduce_fusion.2
  28.5 6.5 %copy.47 = bf16[2048,1024]{0,1:T(8,128)(2,1)} copy(bf16[2048,1024]{1,0:T(8,128)(2,1)} %param.37) | data formatting | bytes 8388608 | tf_op jit(solution)/shard_map/reshape.2
  35.0 0.6 select_reduce_fusion.6
  35.7 0.6 add_compare_fusion
  36.3 0.1 fusion.106
  36.3 0.1 multiply_cosine_fusion
  36.5 13.8 %all-gather.3.cloned.1.call-done = bf16[512,1024]{1,0:T(8,128)(2,1)} async-done(((bf16[32,1024]{1,0:T(8,128)(2,1)}), bf16[512,1024]{1,0:T(8,128)(2,1)}) %all-gather.3.cloned.1.call-update) | async-done | bytes 1048592 | tf_op jit(solution)/shard_map/all_gather | solution.py:104
  50.3 1.5 convolution_convert_fusion.1
  51.8 4.9 %all_gather.22 = bf16[32,2048]{1,0:T(8,128)(2,1)S(1)} all-gather(bf16[32,1024]{1,0:T(8,128)(2,1)S(1)} %convolution_convert_fusion.1), channel_id=1, replica_groups=mesh['seq'=16,'head'=2] {'head'}, dimensions={1}, use_global_device_ids=true | all-gather | bytes 196608 | tf_op jit(solution)/shard_map/all_gather | solution.py:110
  56.8 0.1 convert_reduce_fusion
  56.9 0.2 fusion.26
  57.2 8.5 %fusion.15 = f32[32,3,1024]{2,0,1:T(8,128)S(1)} fusion(bf16[2048,3,1024]{0,2,1:T(8,128)(2,1)} %copy.30, f32[3,1024]{1,0:T(4,128)S(1)} %copy-done.1, bf16[32,2048]{1,0:T(8,128)(2,1)S(1)} %all_gather.22, f32[2048]{0:T(1024)S(1)} %copy-done.5, f32[2048]{0:T(1024)S(1)} %copy-done.6, f32[32]{0:T(128)S(1)} %add_rsqrt_fusion, f32[32]{0:T(128)S(1)} %broadcast_multiply_fusion), kind=kOutput, calls=%fused_computation.22 | convolution fusion | flops 403144704 | bytes 13136128 | tf_op jit(solution)/shard_map/dot_general | solution.py:114
  65.7 0.1 reshape_squeeze.7
  65.9 0.1 slice.84
  66.0 0.1 slice.85
  66.1 0.2 subtract_convert_fusion.1
  66.2 0.3 multiply_reduce_fusion
  66.6 3.4 %fusion.11 = f32[32,4,1,64]{3,2,1,0:T(1,128)S(1)} fusion(bf16[32,8,4,8,256]{4,3,2,1,0:T(8,128)(2,1)} %bitcast.118, bf16[32,4,256,1]{2,1,0,3:T(4,128)(2,1)S(1)} %bitcast.115), kind=kOutput, calls=%fused_computation.16 | convolution fusion | flops 4194304 | bytes 4292608 | tf_op jit(solution)/shard_map/rhc,rthc->rht/dot_general | solution.py:49
  70.0 0.1 fusion.96
  70.1 0.2 fusion.97
  70.3 0.1 select_reduce_fusion.1
  70.4 58.4 %psum.7 = f32[4,4,256]{2,1,0:T(4,128)S(1)} all-reduce(f32[4,4,256]{2,1,0:T(4,128)S(1)} %select_reduce_fusion.1), channel_id=1, replica_groups=mesh['seq'=16,'head'=2] {'seq'}, use_global_device_ids=true, to_apply=%region_8.9 | all-reduce | flops 4096 | bytes 32768 | tf_op jit(solution)/shard_map/psum | solution.py:135
  128.8 0.1 select_reduce_fusion.3
  128.9 3.0 %fusion.108 = f32[4,1,2048]{2,1,0:T(1,128)S(1)} fusion(bf16[2048,4,256]{0,2,1:T(8,128)(2,1)} %bitcast.112, bf16[4,256,1]{1,0,2:T(4,128)(2,1)S(1)} %bitcast.116), kind=kOutput, calls=%fused_computation.149 | convolution fusion | flops 4194304 | bytes 4229120 | tf_op jit(solution)/shard_map/rhc,rthc->rht/dot_general | solution.py:49
  131.9 0.1 fusion.107
  132.0 0.2 fusion.105
  132.3 0.7 fusion.5
  132.9 0.1 broadcast_select_fusion
  133.0 17.8 %all_gather.25 = f32[16,4,4,256]{3,2,1,0:T(4,128)S(1)} all-gather(f32[1,4,4,256]{3,2,1,0:T(4,128)S(1)} %broadcast_select_fusion), channel_id=1, replica_groups=mesh['seq'=16,'head'=2] {'seq'}, dimensions={0}, use_global_device_ids=true | all-gather | bytes 278528 | tf_op jit(solution)/shard_map/all_gather | solution.py:14
  150.9 0.1 broadcast_select_fusion.1
  150.9 19.3 %all_gather.24 = f32[16,4,4]{2,1,0:T(4,128)S(1)} all-gather(f32[1,4,4]{2,1,0:T(4,128)S(1)} %get-tuple-element.228), channel_id=1, replica_groups=mesh['seq'=16,'head'=2] {'seq'}, dimensions={0}, use_global_device_ids=true | all-gather | bytes 1088 | tf_op jit(solution)/shard_map/all_gather | solution.py:14
  170.2 17.7 %all_gather.23 = f32[16,4,4]{2,1,0:T(4,128)S(1)} all-gather(f32[1,4,4]{2,1,0:T(4,128)S(1)} %get-tuple-element.229), channel_id=1, replica_groups=mesh['seq'=16,'head'=2] {'seq'}, dimensions={0}, use_global_device_ids=true | all-gather | bytes 1088 | tf_op jit(solution)/shard_map/all_gather | solution.py:14
  187.9 2.0 while.19
  187.9 0.1 fusion.154
  188.0 0.1 fusion.154
  188.1 0.1 fusion.154
  188.3 0.1 fusion.154
  188.4 0.1 fusion.154
  188.5 0.1 fusion.154
  188.7 0.1 fusion.154
  188.8 0.1 fusion.154
  188.9 0.1 fusion.154
  189.1 0.1 fusion.154
  189.2 0.1 fusion.154
  189.3 0.1 fusion.154
  189.5 0.1 fusion.154
  189.6 0.1 fusion.154
  189.7 0.1 fusion.154
  189.8 0.1 select_reduce_fusion
  189.9 0.1 copy.31
  190.1 3.0 %fusion.8 = f32[32,4,1,256]{3,2,1,0:T(1,128)S(1)} fusion(bf16[32,8,4,8,256]{4,3,2,1,0:T(8,128)(2,1)} %bitcast.113, bf16[32,4,64,1]{2,0,1,3:T(8,128)(2,1)S(1)} %get-tuple-element.218), kind=kOutput, calls=%fused_computation.13 | convolution fusion | flops 4194304 | bytes 4341760 | tf_op jit(solution)/shard_map/rht,rthc->rhc/dot_general | solution.py:56
  193.1 0.1 select_reduce_fusion.5
  193.2 0.1 fusion.93
  193.4 0.1 copy-done
  193.5 0.8 fusion.143
  194.4 10.0 %fusion.14 = bf16[32,2048]{1,0:T(8,128)(2,1)} fusion(f32[32,2048]{1,0:T(8,128)S(1)} %fusion.143, bf16[2048,2048]{1,0:T(8,128)(2,1)} %param.33, bf16[2048,2048]{1,0:T(8,128)(2,1)} %param.31, bf16[32,2048]{1,0:T(8,128)(2,1)S(1)} %all_gather.22, f32[2048]{0:T(1024)S(1)} %copy-done.2, f32[2048]{0:T(1024)S(1)} %copy-done.3, f32[2048]{0:T(1024)S(1)} %copy-done.4, ...), kind=kOutput, calls=%fused_computation.21 | convolution fusion | flops 541720576 | bytes 17326336 | tf_op jit(solution)/shard_map/dot_general | solution.py:193
  204.5 8.8 %reduce-scatter.2.cloned.1.call-done = bf16[32,1024]{1,0:T(8,128)(2,1)} async-done(((bf16[32,2048]{1,0:T(8,128)(2,1)}), bf16[32,1024]{1,0:T(8,128)(2,1)}) %reduce-scatter.2.cloned.1.call-update) | async-done | bytes 65552 | tf_op jit(solution)/shard_map/reduce_scatter | solution.py:196
  213.2 1.5 add_convert_fusion
  214.8 38.6 %all-gather.5.cloned.1.call-done = bf16[512,1024]{1,0:T(8,128)(2,1)} async-done(((bf16[32,1024]{1,0:T(8,128)(2,1)}), bf16[512,1024]{1,0:T(8,128)(2,1)}) %all-gather.5.cloned.1.call-update) | async-done | bytes 1048592 | tf_op jit(solution)/shard_map/all_gather | solution.py:204
  253.4 2.2 convolution_convert_fusion
  (62 shorter events, 0.9 us)
Async XLA Ops:
  6.5 43.8 %all-gather.3.cloned.1.call-start = ((), (), s32[]{:S(2)}) async-start(), calls=%async_computation.1 | async-start | bytes 1114112 | tf_op jit(solution)/shard_map/all_gather | solution.py:104
  7.3 206.0 %reduce-scatter.2.cloned.1.call-start = ((), (), s32[]{:S(2)}) async-start(), calls=%async_computation.2 | async-start | bytes 196608 | tf_op jit(solution)/shard_map/reduce_scatter | solution.py:196
  11.2 17.0 %copy-start.9 = (s32[512]{0:T(512)S(1)}, s32[512]{0:T(512)}, u32[]{:S(2)}) copy-start(s32[512]{0:T(512)} %param.40) | copy-start | bytes 6148
  11.2 17.1 %copy-start.10 = (s32[512]{0:T(512)S(1)}, s32[512]{0:T(512)}, u32[]{:S(2)}) copy-start(s32[512]{0:T(512)} %param.39) | copy-start | bytes 6148
  28.4 28.7 %copy-start.1 = (f32[3,1024]{1,0:T(4,128)S(1)}, f32[3,1024]{1,0:T(4,128)}, u32[]{:S(2)}) copy-start(f32[3,1024]{1,0:T(4,128)} %param.28) | copy-start | bytes 36868
  28.4 28.7 %copy-start.5 = (f32[2048]{0:T(1024)S(1)}, f32[2048]{0:T(1024)}, u32[]{:S(2)}) copy-start(f32[2048]{0:T(1024)} %param.24) | copy-start | bytes 24580
  28.5 28.7 %copy-start.6 = (f32[2048]{0:T(1024)S(1)}, f32[2048]{0:T(1024)}, u32[]{:S(2)}) copy-start(f32[2048]{0:T(1024)} %param.23) | copy-start | bytes 24580
  128.8 3.4 %copy-start.11 = (bf16[2048,1024]{1,0:T(8,128)(2,1)S(1)}, bf16[2048,1024]{1,0:T(8,128)(2,1)}, u32[]{:S(2)}) copy-start(bf16[2048,1024]{1,0:T(8,128)(2,1)} %param.38) | copy-start | bytes 12582916
  190.1 3.5 %copy-start = (bf16[1024,2048]{1,0:T(8,128)(2,1)S(1)}, bf16[1024,2048]{1,0:T(8,128)(2,1)}, u32[]{:S(2)}) copy-start(bf16[1024,2048]{1,0:T(8,128)(2,1)} %param.29) | copy-start | bytes 12582916
  190.1 4.3 %copy-start.2 = (f32[2048]{0:T(1024)S(1)}, f32[2048]{0:T(1024)}, u32[]{:S(2)}) copy-start(f32[2048]{0:T(1024)} %param.32) | copy-start | bytes 24580
  190.1 4.3 %copy-start.3 = (f32[2048]{0:T(1024)S(1)}, f32[2048]{0:T(1024)}, u32[]{:S(2)}) copy-start(f32[2048]{0:T(1024)} %param.26) | copy-start | bytes 24580
  190.1 4.3 %copy-start.4 = (f32[2048]{0:T(1024)S(1)}, f32[2048]{0:T(1024)}, u32[]{:S(2)}) copy-start(f32[2048]{0:T(1024)} %param.25) | copy-start | bytes 24580
  194.4 18.9 %copy-start.7 = (f32[1024]{0:T(1024)S(1)}, f32[1024]{0:T(1024)}, u32[]{:S(2)}) copy-start(f32[1024]{0:T(1024)} %param.34) | copy-start | bytes 12292
  194.4 18.8 %copy-start.8 = (f32[1024]{0:T(1024)S(1)}, f32[1024]{0:T(1024)}, u32[]{:S(2)}) copy-start(f32[1024]{0:T(1024)} %param.30) | copy-start | bytes 12292
  204.4 49.0 %all-gather.5.cloned.1.call-start = ((), (), s32[]{:S(2)}) async-start(), calls=%async_computation.3 | async-start | bytes 1114112 | tf_op jit(solution)/shard_map/all_gather | solution.py:204
Sparse Core Ops, SparseCore 0:
  9.5 40.7 all-gather.2
  204.5 8.6 reduce-scatter.1
  215.4 37.9 all-gather.4
where the time goes:
time: 263 us; the launch traced here: 262 us
  blocking collectives  118 us (45%)
  waiting for transfers between devices  61.9 us (24%)
  matrix products  33 us (13%)
  local copies, waits for them, and re-layouts  25.6 us (10%)
  between operations  16 us (6%)
  other arithmetic  7.06 us (3%)
    psum x1, blocking collectives, local(): long_queries = lax.psum(long_part, 'seq')  58.4 us
    all_gather x3, blocking collectives, merged(): everything = jax.tree.map(lambda part: lax.all_gather(part, axis), array)  54.8 us
    all_gather x1, waiting for transfers between devices, local(): lax.all_gather(finished, 'seq', axis=0, tiled=True)  38.6 us
    unnamed x25, local copies, waits for them, and re-layouts  17.2 us
    all_gather x1, waiting for transfers between devices, local(): shard_rows = lax.all_gather(tokens, 'seq', axis=0, tiled=True)  13.8 us
    dot_general x1, matrix products, local(): jnp.dot(hidden_units, w_down, preferred_element_type=jnp.float32)  9.99 us
    reduce_scatter x1, waiting for transfers between devices, local(): lax.psum_scatter(partial_sum.astype(jnp.bfloat16), 'head', scatter_dimens...  8.76 us
    dot_general x1, matrix products, local(): jnp.dot(normed_attn, w_qkv.reshape(w_qkv.shape[0], 3 * part_width), prefe...  8.47 us
  transfers between devices with their start and end apart: 3, of which 3 were waited for; matrix products, arithmetic and copies ran while one was open for 10% of the time, Pallas kernels for 0%

commit v1 on v0

--- a/solution.py
+++ b/solution.py
@@ -132,7 +132,7 @@
     long_part = jnp.sum(
         jnp.where(long_hits[:, :, None, None], queries.astype(jnp.float32)[:, None], 0.0), axis=0
     )
-    long_queries = lax.psum(long_part, "seq")
+    long_queries = jnp.sum(lax.all_gather(long_part, "seq"), axis=0)
     short_max = keys_short.shape[1]
     short_usable = (jnp.arange(short_max, dtype=jnp.int32)[None, :] < my_lengths[:, None]) & (
         my_lengths <= short_max

time: 263 us -> 225 us (0.86)
  blocking collectives: 118 us -> 79.6 us
    psum x1 -> x0, blocking collectives: 58.4 us -> none  [local(): long_queries = lax.psum(long_part, 'seq')]
    all_gather x0 -> x1, blocking collectives: none -> 20 us  [local(): long_queries = jnp.sum(lax.all_gather(long_part, 'seq'), axis=0)]
  transfers between devices with their start and end apart: 3 -> 3, of which waited for: 3 -> 3; matrix products, arithmetic and copies ran while one was open for 10% -> 12% of each run, Pallas kernels for 0% -> 0%
where the time goes in v1:
time: 225 us; the launch traced here: 224 us
  blocking collectives  79.6 us (35%)
  waiting for transfers between devices  61.9 us (28%)
  matrix products  33 us (15%)
  local copies, waits for them, and re-layouts  25.6 us (11%)
  between operations  16 us (7%)
  other arithmetic  7.15 us (3%)
    all_gather x3, blocking collectives, merged(): everything = jax.tree.map(lambda part: lax.all_gather(part, axis), array)  54.7 us
    all_gather x1, waiting for transfers between devices, local(): lax.all_gather(finished, 'seq', axis=0, tiled=True)  38.6 us
    all_gather x1, blocking collectives, local(): long_queries = jnp.sum(lax.all_gather(long_part, 'seq'), axis=0)  20 us
    unnamed x25, local copies, waits for them, and re-layouts  17.2 us
    all_gather x1, waiting for transfers between devices, local(): shard_rows = lax.all_gather(tokens, 'seq', axis=0, tiled=True)  13.8 us
    dot_general x1, matrix products, local(): jnp.dot(hidden_units, w_down, preferred_element_type=jnp.float32)  9.99 us
    reduce_scatter x1, waiting for transfers between devices, local(): lax.psum_scatter(partial_sum.astype(jnp.bfloat16), 'head', scatter_dimens...  8.73 us
    dot_general x1, matrix products, local(): jnp.dot(normed_attn, w_qkv.reshape(w_qkv.shape[0], 3 * part_width), prefe...  8.47 us
  transfers between devices with their start and end apart: 3, of which 3 were waited for; matrix products, arithmetic and copies ran while one was open for 12% of the time, Pallas kernels for 0%

profile of v1, /device:TPU:0, one launch (start us, length us, event | category | flops | bytes accessed | tf_op | source)
XLA Modules:
  0.0 223.7 jit_solution(15313449590345611683)
XLA Ops:
  6.5 0.7 all-gather.4.cloned.1.call-update
  7.3 1.2 dynamic_slice.37
  11.2 17.0 %copy.30 = bf16[2048,3,1024]{0,2,1:T(8,128)(2,1)} copy(bf16[2048,3,1024]{2,0,1:T(8,128)(2,1)} %param.27) | data formatting | bytes 25165824 | tf_op args[5]
  28.2 0.1 dynamic_slice.36
  28.2 0.2 select_reduce_fusion.2
  28.5 6.5 %copy.47 = bf16[2048,1024]{0,1:T(8,128)(2,1)} copy(bf16[2048,1024]{1,0:T(8,128)(2,1)} %param.37) | data formatting | bytes 8388608 | tf_op jit(solution)/shard_map/reshape.2
  35.0 0.6 select_reduce_fusion.6
  35.7 0.6 add_compare_fusion
  36.3 0.1 fusion.106
  36.3 0.1 multiply_cosine_fusion
  36.5 13.8 %all-gather.4.cloned.1.call-done = bf16[512,1024]{1,0:T(8,128)(2,1)} async-done(((bf16[32,1024]{1,0:T(8,128)(2,1)}), bf16[512,1024]{1,0:T(8,128)(2,1)}) %all-gather.4.cloned.1.call-update) | async-done | bytes 1048592 | tf_op jit(solution)/shard_map/all_gather | solution.py:104
  50.3 1.5 convolution_convert_fusion.1
  51.8 4.9 %all_gather.28 = bf16[32,2048]{1,0:T(8,128)(2,1)S(1)} all-gather(bf16[32,1024]{1,0:T(8,128)(2,1)S(1)} %convolution_convert_fusion.1), channel_id=1, replica_groups=mesh['seq'=16,'head'=2] {'head'}, dimensions={1}, use_global_device_ids=true | all-gather | bytes 196608 | tf_op jit(solution)/shard_map/all_gather | solution.py:110
  56.8 0.1 convert_reduce_fusion
  56.9 0.2 fusion.26
  57.2 8.5 %fusion.15 = f32[32,3,1024]{2,0,1:T(8,128)S(1)} fusion(bf16[2048,3,1024]{0,2,1:T(8,128)(2,1)} %copy.30, f32[3,1024]{1,0:T(4,128)S(1)} %copy-done.1, bf16[32,2048]{1,0:T(8,128)(2,1)S(1)} %all_gather.28, f32[2048]{0:T(1024)S(1)} %copy-done.5, f32[2048]{0:T(1024)S(1)} %copy-done.6, f32[32]{0:T(128)S(1)} %add_rsqrt_fusion, f32[32]{0:T(128)S(1)} %broadcast_multiply_fusion), kind=kOutput, calls=%fused_computation.22 | convolution fusion | flops 403144704 | bytes 13136128 | tf_op jit(solution)/shard_map/dot_general | solution.py:114
  65.7 0.1 reshape_squeeze.7
  65.9 0.1 slice.84
  66.0 0.1 slice.85
  66.1 0.2 subtract_convert_fusion.1
  66.2 0.3 multiply_reduce_fusion
  66.6 3.4 %fusion.11 = f32[32,4,1,64]{3,2,1,0:T(1,128)S(1)} fusion(bf16[32,8,4,8,256]{4,3,2,1,0:T(8,128)(2,1)} %bitcast.120, bf16[32,4,256,1]{2,1,0,3:T(4,128)(2,1)S(1)} %bitcast.117), kind=kOutput, calls=%fused_computation.16 | convolution fusion | flops 4194304 | bytes 4292608 | tf_op jit(solution)/shard_map/rhc,rthc->rht/dot_general | solution.py:49
  70.0 0.1 fusion.96
  70.1 0.2 fusion.97
  70.3 0.1 select_reduce_fusion.1
  70.4 20.0 %all-gather = f32[64,4,256]{2,1,0:T(4,128)S(1)} all-gather(f32[4,4,256]{2,1,0:T(4,128)S(1)} %select_reduce_fusion.1), channel_id=2, replica_groups=mesh['seq'=16,'head'=2] {'seq'}, dimensions={0}, use_global_device_ids=true | all-gather | bytes 278528 | tf_op jit(solution)/shard_map/all_gather | solution.py:135
  90.5 0.1 select_reduce_fusion.3
  90.6 3.0 %fusion.108 = f32[4,1,2048]{2,1,0:T(1,128)S(1)} fusion(bf16[2048,4,256]{0,2,1:T(8,128)(2,1)} %bitcast.113, bf16[4,256,1]{1,0,2:T(4,128)(2,1)S(1)} %bitcast.118), kind=kOutput, calls=%fused_computation.149 | convolution fusion | flops 4194304 | bytes 4229120 | tf_op jit(solution)/shard_map/rhc,rthc->rht/dot_general | solution.py:49
  93.6 0.1 fusion.107
  93.7 0.2 fusion.105
  93.9 0.7 fusion.5
  94.6 0.1 broadcast_select_fusion
  94.7 18.1 %all_gather.33 = f32[16,4,4,256]{3,2,1,0:T(4,128)S(1)} all-gather(f32[1,4,4,256]{3,2,1,0:T(4,128)S(1)} %broadcast_select_fusion), channel_id=1, replica_groups=mesh['seq'=16,'head'=2] {'seq'}, dimensions={0}, use_global_device_ids=true | all-gather | bytes 278528 | tf_op jit(solution)/shard_map/all_gather | solution.py:14
  112.8 0.1 broadcast_select_fusion.1
  112.9 18.8 %all_gather.32 = f32[16,4,4]{2,1,0:T(4,128)S(1)} all-gather(f32[1,4,4]{2,1,0:T(4,128)S(1)} %get-tuple-element.228), channel_id=1, replica_groups=mesh['seq'=16,'head'=2] {'seq'}, dimensions={0}, use_global_device_ids=true | all-gather | bytes 1088 | tf_op jit(solution)/shard_map/all_gather | solution.py:14
  131.7 17.7 %all_gather.31 = f32[16,4,4]{2,1,0:T(4,128)S(1)} all-gather(f32[1,4,4]{2,1,0:T(4,128)S(1)} %get-tuple-element.229), channel_id=1, replica_groups=mesh['seq'=16,'head'=2] {'seq'}, dimensions={0}, use_global_device_ids=true | all-gather | bytes 1088 | tf_op jit(solution)/shard_map/all_gather | solution.py:14
  149.4 2.0 while.19
  149.4 0.1 fusion.154
  149.6 0.1 fusion.154
  149.7 0.1 fusion.154
  149.8 0.1 fusion.154
  150.0 0.1 fusion.154
  150.1 0.1 fusion.154
  150.2 0.1 fusion.154
  150.4 0.1 fusion.154
  150.5 0.1 fusion.154
  150.6 0.1 fusion.154
  150.8 0.1 fusion.154
  150.9 0.1 fusion.154
  151.1 0.1 fusion.154
  151.2 0.1 fusion.154
  151.3 0.1 fusion.154
  151.4 0.1 select_reduce_fusion
  151.5 0.1 copy.31
  151.7 3.0 %fusion.8 = f32[32,4,1,256]{3,2,1,0:T(1,128)S(1)} fusion(bf16[32,8,4,8,256]{4,3,2,1,0:T(8,128)(2,1)} %bitcast.114, bf16[32,4,64,1]{2,0,1,3:T(8,128)(2,1)S(1)} %get-tuple-element.218), kind=kOutput, calls=%fused_computation.13 | convolution fusion | flops 4194304 | bytes 4341760 | tf_op jit(solution)/shard_map/rht,rthc->rhc/dot_general | solution.py:56
  154.7 0.1 select_reduce_fusion.5
  154.8 0.1 fusion.93
  155.0 0.1 copy-done
  155.1 0.8 fusion.143
  156.0 10.0 %fusion.14 = bf16[32,2048]{1,0:T(8,128)(2,1)} fusion(f32[32,2048]{1,0:T(8,128)S(1)} %fusion.143, bf16[2048,2048]{1,0:T(8,128)(2,1)} %param.33, bf16[2048,2048]{1,0:T(8,128)(2,1)} %param.31, bf16[32,2048]{1,0:T(8,128)(2,1)S(1)} %all_gather.28, f32[2048]{0:T(1024)S(1)} %copy-done.2, f32[2048]{0:T(1024)S(1)} %copy-done.3, f32[2048]{0:T(1024)S(1)} %copy-done.4, ...), kind=kOutput, calls=%fused_computation.21 | convolution fusion | flops 541720576 | bytes 17326336 | tf_op jit(solution)/shard_map/dot_general | solution.py:193
  166.1 8.7 %reduce-scatter.2.cloned.1.call-done = bf16[32,1024]{1,0:T(8,128)(2,1)} async-done(((bf16[32,2048]{1,0:T(8,128)(2,1)}), bf16[32,1024]{1,0:T(8,128)(2,1)}) %reduce-scatter.2.cloned.1.call-update) | async-done | bytes 65552 | tf_op jit(solution)/shard_map/reduce_scatter | solution.py:196
  174.8 1.5 add_convert_fusion
  176.3 38.6 %all-gather.6.cloned.1.call-done = bf16[512,1024]{1,0:T(8,128)(2,1)} async-done(((bf16[32,1024]{1,0:T(8,128)(2,1)}), bf16[512,1024]{1,0:T(8,128)(2,1)}) %all-gather.6.cloned.1.call-update) | async-done | bytes 1048592 | tf_op jit(solution)/shard_map/all_gather | solution.py:204
  214.9 2.2 convolution_convert_fusion
  (63 shorter events, 1.0 us)
Async XLA Ops:
  6.5 43.8 %all-gather.4.cloned.1.call-start = ((), (), s32[]{:S(2)}) async-start(), calls=%async_computation.1 | async-start | bytes 1114112 | tf_op jit(solution)/shard_map/all_gather | solution.py:104
  7.3 167.5 %reduce-scatter.2.cloned.1.call-start = ((), (), s32[]{:S(2)}) async-start(), calls=%async_computation.2 | async-start | bytes 196608 | tf_op jit(solution)/shard_map/reduce_scatter | solution.py:196
  11.2 17.0 %copy-start.9 = (s32[512]{0:T(512)S(1)}, s32[512]{0:T(512)}, u32[]{:S(2)}) copy-start(s32[512]{0:T(512)} %param.40) | copy-start | bytes 6148
  11.2 17.1 %copy-start.10 = (s32[512]{0:T(512)S(1)}, s32[512]{0:T(512)}, u32[]{:S(2)}) copy-start(s32[512]{0:T(512)} %param.39) | copy-start | bytes 6148
  28.4 28.7 %copy-start.1 = (f32[3,1024]{1,0:T(4,128)S(1)}, f32[3,1024]{1,0:T(4,128)}, u32[]{:S(2)}) copy-start(f32[3,1024]{1,0:T(4,128)} %param.28) | copy-start | bytes 36868
  28.4 28.7 %copy-start.5 = (f32[2048]{0:T(1024)S(1)}, f32[2048]{0:T(1024)}, u32[]{:S(2)}) copy-start(f32[2048]{0:T(1024)} %param.24) | copy-start | bytes 24580
  28.5 28.7 %copy-start.6 = (f32[2048]{0:T(1024)S(1)}, f32[2048]{0:T(1024)}, u32[]{:S(2)}) copy-start(f32[2048]{0:T(1024)} %param.23) | copy-start | bytes 24580
  90.5 3.4 %copy-start.11 = (bf16[2048,1024]{1,0:T(8,128)(2,1)S(1)}, bf16[2048,1024]{1,0:T(8,128)(2,1)}, u32[]{:S(2)}) copy-start(bf16[2048,1024]{1,0:T(8,128)(2,1)} %param.38) | copy-start | bytes 12582916
  151.7 3.5 %copy-start = (bf16[1024,2048]{1,0:T(8,128)(2,1)S(1)}, bf16[1024,2048]{1,0:T(8,128)(2,1)}, u32[]{:S(2)}) copy-start(bf16[1024,2048]{1,0:T(8,128)(2,1)} %param.29) | copy-start | bytes 12582916
  151.7 4.3 %copy-start.2 = (f32[2048]{0:T(1024)S(1)}, f32[2048]{0:T(1024)}, u32[]{:S(2)}) copy-start(f32[2048]{0:T(1024)} %param.32) | copy-start | bytes 24580
  151.7 4.3 %copy-start.3 = (f32[2048]{0:T(1024)S(1)}, f32[2048]{0:T(1024)}, u32[]{:S(2)}) copy-start(f32[2048]{0:T(1024)} %param.26) | copy-start | bytes 24580
  151.7 4.3 %copy-start.4 = (f32[2048]{0:T(1024)S(1)}, f32[2048]{0:T(1024)}, u32[]{:S(2)}) copy-start(f32[2048]{0:T(1024)} %param.25) | copy-start | bytes 24580
  156.0 18.8 %copy-start.7 = (f32[1024]{0:T(1024)S(1)}, f32[1024]{0:T(1024)}, u32[]{:S(2)}) copy-start(f32[1024]{0:T(1024)} %param.34) | copy-start | bytes 12292
  156.0 18.8 %copy-start.8 = (f32[1024]{0:T(1024)S(1)}, f32[1024]{0:T(1024)}, u32[]{:S(2)}) copy-start(f32[1024]{0:T(1024)} %param.30) | copy-start | bytes 12292
  166.0 48.9 %all-gather.6.cloned.1.call-start = ((), (), s32[]{:S(2)}) async-start(), calls=%async_computation.3 | async-start | bytes 1114112 | tf_op jit(solution)/shard_map/all_gather | solution.py:204
Sparse Core Ops, SparseCore 0:
  9.5 40.7 all-gather.3
  166.1 8.6 reduce-scatter.1
  177.0 37.9 all-gather.5
